TPU v7x, 128 devices: a whole 4x4x4 slice. The times are simulated.
128 devices in a mesh: rep: 16 (over x, z), grp: 8 (over y, core).
Axes of the slice: x: 4, y: 4, z: 4, core: 2. Of those that a mesh axis runs over, the one named last changes fastest.
Arguments:
- inputs: bfloat16 [2, 262144, 1152], P(None, ('rep', 'grp')), may hold values from -6 to 6
- out_grads: bfloat16 [2, 262144, 1152], P(None, ('rep', 'grp')), may hold values from -6 to 6
- weights: bfloat16 [2, 1152, 1152], P(None, 'grp'), may hold values from -3 to 3
- biases: bfloat16 [2, 1152], P(None, 'grp'), may hold values from -3 to 3
- errors: float32 [16, 2, 1152, 1152], P('rep', None, 'grp'), may hold values from -6 to 6
- momenta: float32 [2, 1152, 1152], P(None, 'grp'), may hold values from -3 to 3
- bias_momenta: float32 [2, 1152], P(None, 'grp'), may hold values from -3 to 3
- q_start: float32 [2, 1152, 32], replicated, may hold values from -6 to 6
Outputs:
- new_weights: bfloat16 [2, 1152, 1152], replicated
- new_biases: bfloat16 [2, 1152], replicated
- new_errors: float32 [16, 2, 1152, 1152], P('rep', None, 'grp')
- new_momenta: float32 [2, 1152, 1152], P(None, 'grp')
- new_bias_momenta: float32 [2, 1152], P(None, 'grp')
All inputs are finite; a program needn't handle non-finite values.
Results may differ from a plain program's by a relative error of at most 0.0045.
Values may be sent and summed in bfloat16 or wider, within the bound.
No kernel may reach another device: no remote copies, remote signals or barrier semaphores. Data moves between devices by JAX's collectives and lax.ppermute only.
A program may use at most 256 MiB of HBM per device.

v0:
```python
import jax
import jax.numpy as jnp
from jax import lax
from jax.sharding import PartitionSpec as P

ROUNDS = 2
NS_STEPS = 5
HIGH = lax.Precision.HIGHEST


def orthonormal(p_sum, gram):
    fro = jnp.sqrt(jnp.sum(gram * gram, axis=(1, 2))) + 1e-06
    scaled = gram / fro[:, None, None]
    eye = jnp.eye(gram.shape[-1], dtype=jnp.float32)
    ymat = scaled
    zmat = jnp.broadcast_to(eye, gram.shape)
    for step in range(NS_STEPS):
        tmat = 1.5 * eye - 0.5 * jnp.einsum("lab,lbc->lac", zmat, ymat, precision=HIGH)
        ymat = jnp.einsum("lab,lbc->lac", ymat, tmat, precision=HIGH)
        zmat = jnp.einsum("lab,lbc->lac", tmat, zmat, precision=HIGH)
    phat = jnp.einsum("lrk,lkj->lrj", p_sum, zmat, precision=HIGH)
    return phat / jnp.sqrt(fro)[:, None, None]


def body(inputs, out_grads, weights, biases, errors, momenta, bias_momenta, q_start):
    layers = inputs.shape[0]
    tok = inputs.shape[1]
    width = inputs.shape[2]
    groups = lax.axis_size("grp")
    reps = lax.axis_size("rep")
    rows = width // groups
    scale = float(tok) ** (-0.5)
    grads = []
    for layer in range(layers):
        x_layer = inputs[layer]
        y_layer = out_grads[layer]

        def term(start, count, x_layer=x_layer, y_layer=y_layer):
            return jnp.einsum("tr,te->re", x_layer, y_layer, preferred_element_type=jnp.float32)

        grads.append(
            lax.psum_scatter(
                term(jnp.int32(0), lax.axis_size("grp") * rows),
                "grp",
                scatter_dimension=0,
                tiled=True,
            )
        )
    merged = jnp.stack(grads) * scale + errors[0]
    col_sums = jnp.sum(out_grads, axis=1, dtype=jnp.float32)
    bias_total = lax.psum(col_sums, ("rep", "grp")) * (scale / reps)
    bias_rows = biases.shape[1]
    bias_grad = lax.dynamic_slice_in_dim(
        bias_total, lax.axis_index("grp") * bias_rows, bias_rows, 1
    )
    qmat = q_start
    phat = None
    for rnd in range(ROUNDS):
        local_p = jnp.einsum("lre,lek->lrk", merged, qmat, precision=HIGH)
        p_sum = lax.psum(local_p, "rep")
        local_gram = jnp.einsum("lrk,lrj->lkj", p_sum, p_sum, precision=HIGH)
        gram = lax.psum(local_gram, "grp")
        phat = orthonormal(p_sum, gram)
        local_q = jnp.einsum("lre,lrk->lek", merged, phat, precision=HIGH)
        qmat = lax.psum(local_q, ("rep", "grp"))
    approx = jnp.einsum("lrk,lek->lre", phat, qmat, precision=HIGH) / reps
    new_errors = (merged - approx)[None]
    new_momenta = 0.9 * momenta + approx
    weight_shard = (weights.astype(jnp.float32) - 0.5 * new_momenta).astype(jnp.bfloat16)
    new_bias_momenta = 0.9 * bias_momenta + bias_grad
    bias_shard = (biases.astype(jnp.float32) - 0.5 * new_bias_momenta).astype(jnp.bfloat16)
    new_weights, new_biases = (
        lax.all_gather(weight_shard, "grp", axis=1, tiled=True),
        lax.all_gather(bias_shard, "grp", axis=1, tiled=True),
    )
    return (new_weights, new_biases, new_errors, new_momenta, new_bias_momenta)


def solution(mesh):
    placed = (
        P(None, ("rep", "grp"), None),
        P(None, ("rep", "grp"), None),
        P(None, "grp", None),
        P(None, "grp"),
        P("rep", None, "grp", None),
        P(None, "grp", None),
        P(None, "grp"),
        P(),
    )
    return jax.shard_map(
        body,
        mesh=mesh,
        in_specs=placed,
        out_specs=(P(), P(), P("rep", None, "grp", None), P(None, "grp", None), P(None, "grp")),
        check_vma=False,
    )
```

profile of v0, /device:TPU:1, one launch (start us, length us, event | category | flops | bytes accessed | tf_op | source)
XLA Modules:
  0.0 687.0 jit_solution(1677941259270240270)
XLA Ops:
  7.2 12.5 %fusion.3 = f32[1152,1152]{1,0:T(8,128)} fusion(bf16[2,2048,1152]{2,1,0:T(8,128)(2,1)} %param.9, bf16[2,2048,1152]{2,1,0:T(8,128)(2,1)} %param.8), kind=kOutput, calls=%fused_computation.4 | convolution fusion | flops 5435817984 | bytes 14745600 | tf_op jit(solution)/shard_map/tr,te->re/dot_general | solution.py:39
  19.7 0.2 reduce-scatter.5.cloned.1.call-start
  19.9 12.5 %fusion = f32[1152,1152]{1,0:T(8,128)} fusion(bf16[2,2048,1152]{2,1,0:T(8,128)(2,1)} %param.9, bf16[2,2048,1152]{2,1,0:T(8,128)(2,1)} %param.8), kind=kOutput, calls=%fused_computation.1 | convolution fusion | flops 5435817984 | bytes 14745600 | tf_op jit(solution)/shard_map/tr,te->re/dot_general | solution.py:39
  32.6 28.2 %reduce-scatter.3.cloned.1.call-done = f32[144,1152]{1,0:T(8,128)} async-done(((f32[1152,1152]{1,0:T(8,128)}), f32[144,1152]{1,0:T(8,128)}) %reduce-scatter.3.cloned.1.call-update) | async-done | bytes 663568 | tf_op jit(solution)/shard_map/reduce_scatter | solution.py:42
  60.7 42.6 %reduce-scatter.5.cloned.1.call-done = f32[144,1152]{1,0:T(8,128)} async-done(((f32[1152,1152]{1,0:T(8,128)}), f32[144,1152]{1,0:T(8,128)}) %reduce-scatter.5.cloned.1.call-update) | async-done | bytes 663568 | tf_op jit(solution)/shard_map/reduce_scatter | solution.py:42
  103.3 1.4 fusion.10
  104.8 1.5 fusion.36
  106.3 60.4 %psum.49 = f32[2,144,32]{1,2,0:T(8,128)S(1)} all-reduce(f32[2,144,32]{1,2,0:T(8,128)S(1)} %fusion.36), channel_id=1, replica_groups=mesh['rep'=16,'grp'=8] {'rep'}, use_global_device_ids=true, to_apply=%region_2.0 | all-reduce | flops 9216 | bytes 73728 | tf_op jit(solution)/shard_map/psum | solution.py:60
  166.7 0.2 fusion.37
  166.9 37.5 %psum.50 = f32[2,32,32]{2,1,0:T(8,128)S(1)} all-reduce(f32[2,32,32]{2,1,0:T(8,128)S(1)} %fusion.37), channel_id=1, replica_groups=mesh['rep'=16,'grp'=8] {'grp'}, use_global_device_ids=true, to_apply=%region_3.0 | all-reduce | flops 2048 | bytes 16384 | tf_op jit(solution)/shard_map/psum | solution.py:62
  204.4 0.2 fusion.20
  204.7 0.2 fusion.29
  205.1 0.2 fusion.19
  205.3 0.2 fusion.39
  205.5 0.2 fusion.38
  205.6 0.2 fusion.18
  205.8 0.2 fusion.41
  206.0 0.2 fusion.40
  206.1 0.2 fusion.17
  206.6 0.2 fusion.16
  206.8 0.2 fusion.44
  207.0 0.2 convolution_divide_fusion.1
  207.2 1.6 fusion.45
  208.9 139.4 %all-reduce.3.cloned.1.call-done = f32[2,1152,32]{1,2,0:T(8,128)} async-done(((f32[2,1152,32]{1,2,0:T(8,128)}), f32[2,1152,32]{1,2,0:T(8,128)}) %all-reduce.3.cloned.1.call-update) | async-done | bytes 294928 | tf_op jit(solution)/shard_map/psum | solution.py:65
  348.4 2.5 fusion.46
  350.9 58.2 %psum.52 = f32[2,144,32]{1,2,0:T(8,128)S(1)} all-reduce(f32[2,144,32]{1,2,0:T(8,128)S(1)} %fusion.46), channel_id=1, replica_groups=mesh['rep'=16,'grp'=8] {'rep'}, use_global_device_ids=true, to_apply=%region_6.0 | all-reduce | flops 9216 | bytes 73728 | tf_op jit(solution)/shard_map/psum | solution.py:60
  409.1 0.2 fusion.47
  409.3 35.9 %psum.53 = f32[2,32,32]{2,1,0:T(8,128)S(1)} all-reduce(f32[2,32,32]{2,1,0:T(8,128)S(1)} %fusion.47), channel_id=1, replica_groups=mesh['rep'=16,'grp'=8] {'grp'}, use_global_device_ids=true, to_apply=%region_7.0 | all-reduce | flops 2048 | bytes 16384 | tf_op jit(solution)/shard_map/psum | solution.py:62
  445.3 0.2 fusion.15
  445.6 0.2 fusion.30
  446.0 0.2 fusion.14
  446.2 0.2 fusion.49
  446.3 0.2 fusion.48
  446.5 0.2 fusion.13
  447.0 0.2 fusion.12
  447.4 0.2 fusion.52
  447.5 0.2 fusion.11
  447.7 0.2 fusion.54
  448.0 0.2 convolution_divide_fusion
  448.2 1.6 fusion.55
  449.8 139.4 %all-reduce.5.cloned.1.call-done = f32[2,1152,32]{1,2,0:T(8,128)} async-done(((f32[2,1152,32]{1,2,0:T(8,128)}), f32[2,1152,32]{1,2,0:T(8,128)}) %all-reduce.5.cloned.1.call-update) | async-done | bytes 294928 | tf_op jit(solution)/shard_map/psum | solution.py:65
  589.2 4.4 subtract_convert_fusion
  593.7 5.0 convert_reduce_fusion
  598.7 65.3 %psum.55 = f32[2,1152]{1,0:T(2,128)S(1)} all-reduce(f32[2,1152]{1,0:T(2,128)S(1)} %convert_reduce_fusion), channel_id=1, replica_groups=mesh['rep'=16,'grp'=8] {'rep','grp'}, use_global_device_ids=true, to_apply=%region_11.0 | all-reduce | flops 2304 | bytes 18432 | tf_op jit(solution)/shard_map/psum | solution.py:51
  664.0 0.7 fusion.32
  664.6 9.9 %all-gather = bf16[8,144,2]{1,2,0:T(2,128)(2,1)S(1)} all-gather(bf16[1,144,2]{1,2,0:T(2,128)(2,1)S(1)} %get-tuple-element.5), channel_id=1, replica_groups=mesh['rep'=16,'grp'=8] {'grp'}, dimensions={0}, use_global_device_ids=true | all-gather | bytes 5184 | tf_op jit(solution)/shard_map/all_gather | solution.py:74
  674.5 0.7 reshape.33
  675.2 5.3 copy.22
  (34 shorter events, 1.6 us)
Async XLA Ops:
  7.2 97.6 %copy-start = (f32[2,1152,32]{1,2,0:T(8,128)S(1)}, f32[2,1152,32]{1,2,0:T(8,128)}, u32[]{:S(2)}) copy-start(f32[2,1152,32]{1,2,0:T(8,128)} %param.15) | copy-start | bytes 884740
  7.2 53.5 %reduce-scatter.3.cloned.1.call-start = ((), (), s32[]{:S(2)}) async-start(), calls=%async_computation.2 | async-start | bytes 5971968 | tf_op jit(solution)/shard_map/reduce_scatter | solution.py:42
  19.7 83.6 %reduce-scatter.5.cloned.1.call-start = ((), (), s32[]{:S(2)}) async-start(), calls=%async_computation.3 | async-start | bytes 5971968 | tf_op jit(solution)/shard_map/reduce_scatter | solution.py:42
  32.5 70.8 %copy-start.1 = (f32[1,2,144,1152]{3,2,1,0:T(8,128)S(1)}, f32[1,2,144,1152]{3,2,1,0:T(8,128)}, u32[]{:S(2)}) copy-start(f32[1,2,144,1152]{3,2,1,0:T(8,128)} %param.12) | copy-start | bytes 3981316
  32.5 315.9 %all-reduce.3.cloned.1.call-start = ((), (), s32[]{:S(2)}) async-start(), calls=%async_computation.4 | async-start | bytes 589824 | tf_op jit(solution)/shard_map/psum | solution.py:65
  208.9 380.4 %all-reduce.5.cloned.1.call-start = ((), (), s32[]{:S(2)}) async-start(), calls=%async_computation.5 | async-start | bytes 589824 | tf_op jit(solution)/shard_map/psum | solution.py:65
  447.2 142.1 %copy-start.2 = (f32[2,144,1152]{2,1,0:T(8,128)S(1)}, f32[2,144,1152]{2,1,0:T(8,128)}, u32[]{:S(2)}) copy-start(f32[2,144,1152]{2,1,0:T(8,128)} %param.13) | copy-start | bytes 3981316
  449.8 225.4 %all-gather.3.cloned.1.call-start = ((), (), s32[]{:S(2)}) async-start(), calls=%async_computation.6 | async-start | bytes 5971968 | tf_op jit(solution)/shard_map/all_gather | solution.py:73
  593.7 70.3 %copy-start.3 = (f32[2,144]{1,0:T(2,128)S(1)}, f32[2,144]{1,0:T(2,128)}, u32[]{:S(2)}) copy-start(f32[2,144]{1,0:T(2,128)} %param.14) | copy-start | bytes 3460
  593.7 70.2 %copy-start.4 = (bf16[2,144]{1,0:T(2,128)(2,1)S(1)}, bf16[2,144]{1,0:T(2,128)(2,1)}, u32[]{:S(2)}) copy-start(bf16[2,144]{1,0:T(2,128)(2,1)} %param.11) | copy-start | bytes 1732
Sparse Core Ops, SparseCore 0:
  19.8 40.8 reduce-scatter.2
  63.7 39.5 reduce-scatter.4
  209.0 139.3 all-reduce.2
  449.9 139.3 all-reduce.4
  593.8 36.2 all-gather.2
where the time goes:
time: 687 us
  waiting for transfers between devices  350 us (51%)
  blocking collectives  267 us (39%)
  matrix products  42.4 us (6%)
  between operations  14.1 us (2%)
  other arithmetic  7.32 us (1%)
    psum x2, waiting for transfers between devices, body(): qmat = lax.psum(local_q, ('rep', 'grp'))  279 us
    psum x2, blocking collectives, body(): p_sum = lax.psum(local_p, 'rep')  119 us
    psum x2, blocking collectives, body(): gram = lax.psum(local_gram, 'grp')  73.4 us
    reduce_scatter x2, waiting for transfers between devices, body(): lax.psum_scatter(term(jnp.int32(0), lax.axis_size('grp') * rows), 'grp',...  70.7 us
    psum x1, blocking collectives, body(): bias_total = lax.psum(col_sums, ('rep', 'grp')) * (scale / reps)  65.3 us
    dot_general x2, matrix products, term(): jnp.einsum('tr,te->re', x_layer, y_layer, preferred_element_type=jnp.floa...  25 us
  transfers between devices with their start and end apart: 5, of which 4 were waited for; matrix products, arithmetic and copies ran while one was open for 3% of the time, Pallas kernels for 0%

commit v1 on v0

--- a/solution.py
+++ b/solution.py
@@ -48,7 +48,7 @@
         )
     merged = jnp.stack(grads) * scale + errors[0]
     col_sums = jnp.sum(out_grads, axis=1, dtype=jnp.float32)
-    bias_total = lax.psum(col_sums, ("rep", "grp")) * (scale / reps)
+    bias_total = lax.psum(lax.psum(col_sums, "rep"), "grp") * (scale / reps)
     bias_rows = biases.shape[1]
     bias_grad = lax.dynamic_slice_in_dim(
         bias_total, lax.axis_index("grp") * bias_rows, bias_rows, 1

time: 687 us -> 643 us (0.936)
  blocking collectives: 267 us -> 204 us
  waiting for transfers between devices: 350 us -> 368 us
    psum x1 -> x0, blocking collectives: 65.3 us -> none  [body(): bias_total = lax.psum(col_sums, ('rep', 'grp')) * (scale / reps)]
    all_gather x1, waiting for transfers between devices: 0.01 us -> 23.3 us  [body(): lax.all_gather(weight_shard, 'grp', axis=1, tiled=True)]
  transfers between devices with their start and end apart: 5 -> 5, of which waited for: 4 -> 5; matrix products, arithmetic and copies ran while one was open for 3% -> 3% of each run, Pallas kernels for 0% -> 0%
where the time goes in v1:
time: 643 us
  waiting for transfers between devices  368 us (57%)
  blocking collectives  204 us (32%)
  matrix products  42.4 us (7%)
  between operations  14.1 us (2%)
  other arithmetic  7.31 us (1%)
    psum x2, waiting for transfers between devices, body(): qmat = lax.psum(local_q, ('rep', 'grp'))  275 us
    psum x2, blocking collectives, body(): p_sum = lax.psum(local_p, 'rep')  119 us
    psum x2, blocking collectives, body(): gram = lax.psum(local_gram, 'grp')  73.9 us
    reduce_scatter x2, waiting for transfers between devices, body(): lax.psum_scatter(term(jnp.int32(0), lax.axis_size('grp') * rows), 'grp',...  70.2 us
    dot_general x2, matrix products, term(): jnp.einsum('tr,te->re', x_layer, y_layer, preferred_element_type=jnp.floa...  25 us
    all_gather x1, waiting for transfers between devices, body(): lax.all_gather(weight_shard, 'grp', axis=1, tiled=True)  23.3 us
  transfers between devices with their start and end apart: 5, of which 5 were waited for; matrix products, arithmetic and copies ran while one was open for 3% of the time, Pallas kernels for 0%

profile of v1, /device:TPU:1, one launch (start us, length us, event | category | flops | bytes accessed | tf_op | source)
XLA Modules:
  0.0 642.9 jit_solution(10488776412623918732)
XLA Ops:
  7.2 12.5 %fusion = f32[1152,1152]{1,0:T(8,128)} fusion(bf16[2,2048,1152]{2,1,0:T(8,128)(2,1)} %param.9, bf16[2,2048,1152]{2,1,0:T(8,128)(2,1)} %param.8), kind=kOutput, calls=%fused_computation.1 | convolution fusion | flops 5435817984 | bytes 14745600 | tf_op jit(solution)/shard_map/tr,te->re/dot_general | solution.py:39
  19.8 0.2 reduce-scatter.3.cloned.1.call-start
  20.0 12.4 %fusion.3 = f32[1152,1152]{1,0:T(8,128)} fusion(bf16[2,2048,1152]{2,1,0:T(8,128)(2,1)} %param.9, bf16[2,2048,1152]{2,1,0:T(8,128)(2,1)} %param.8), kind=kOutput, calls=%fused_computation.4 | convolution fusion | flops 5435817984 | bytes 14745600 | tf_op jit(solution)/shard_map/tr,te->re/dot_general | solution.py:39
  32.6 28.2 %reduce-scatter.5.cloned.1.call-done = f32[144,1152]{1,0:T(8,128)} async-done(((f32[1152,1152]{1,0:T(8,128)}), f32[144,1152]{1,0:T(8,128)}) %reduce-scatter.5.cloned.1.call-update) | async-done | bytes 663568 | tf_op jit(solution)/shard_map/reduce_scatter | solution.py:42
  60.8 42.0 %reduce-scatter.3.cloned.1.call-done = f32[144,1152]{1,0:T(8,128)} async-done(((f32[1152,1152]{1,0:T(8,128)}), f32[144,1152]{1,0:T(8,128)}) %reduce-scatter.3.cloned.1.call-update) | async-done | bytes 663568 | tf_op jit(solution)/shard_map/reduce_scatter | solution.py:42
  102.8 1.4 fusion.10
  104.3 1.5 fusion.36
  105.8 60.4 %psum.56 = f32[2,144,32]{1,2,0:T(8,128)S(1)} all-reduce(f32[2,144,32]{1,2,0:T(8,128)S(1)} %fusion.36), channel_id=1, replica_groups=mesh['rep'=16,'grp'=8] {'rep'}, use_global_device_ids=true, to_apply=%region_2.0 | all-reduce | flops 9216 | bytes 73728 | tf_op jit(solution)/shard_map/psum | solution.py:60
  166.2 0.2 fusion.37
  166.4 37.5 %psum.57 = f32[2,32,32]{2,1,0:T(8,128)S(1)} all-reduce(f32[2,32,32]{2,1,0:T(8,128)S(1)} %fusion.37), channel_id=1, replica_groups=mesh['rep'=16,'grp'=8] {'grp'}, use_global_device_ids=true, to_apply=%region_3.0 | all-reduce | flops 2048 | bytes 16384 | tf_op jit(solution)/shard_map/psum | solution.py:62
  203.9 0.2 fusion.20
  204.2 0.2 fusion.29
  204.6 0.2 fusion.19
  204.8 0.2 fusion.39
  204.9 0.2 fusion.38
  205.1 0.2 fusion.18
  205.3 0.2 fusion.41
  205.5 0.2 fusion.40
  205.6 0.2 fusion.17
  206.1 0.2 fusion.16
  206.3 0.2 fusion.44
  206.5 0.2 convolution_divide_fusion.1
  206.7 1.6 fusion.45
  208.4 0.3 all-reduce.7.cloned.1.call-start
  208.6 5.0 convert_reduce_fusion
  213.6 134.3 %all-reduce.5.cloned.1.call-done = f32[2,1152,32]{1,2,0:T(8,128)} async-done(((f32[2,1152,32]{1,2,0:T(8,128)}), f32[2,1152,32]{1,2,0:T(8,128)}) %all-reduce.5.cloned.1.call-update) | async-done | bytes 294928 | tf_op jit(solution)/shard_map/psum | solution.py:65
  347.9 2.5 fusion.46
  350.4 59.0 %all-reduce = (f32[2,144,32]{1,2,0:T(8,128)S(1)}, f32[2,1152]{1,0:T(2,128)S(1)}) all-reduce(f32[2,144,32]{1,2,0:T(8,128)S(1)} %fusion.46, f32[2,1152]{1,0:T(2,128)S(1)} %convert_reduce_fusion), channel_id=1, replica_groups=mesh['rep'=16,'grp'=8] {'rep'}, use_global_device_ids=true, to_apply=%region_6.0 | all-reduce | flops 11520 | bytes 92160 | tf_op jit(solution)/shard_map/psum | solution.py:60
  409.4 0.2 fusion.47
  409.6 36.5 %all-reduce.1 = (f32[2,32,32]{2,1,0:T(8,128)S(1)}, f32[2,1152]{1,0:T(2,128)S(1)}) all-reduce(f32[2,32,32]{2,1,0:T(8,128)S(1)} %fusion.47, f32[2,1152]{1,0:T(2,128)S(1)} %get-tuple-element.6), channel_id=1, replica_groups=mesh['rep'=16,'grp'=8] {'grp'}, use_global_device_ids=true, to_apply=%region_7.0 | all-reduce | flops 4352 | bytes 34816 | tf_op jit(solution)/shard_map/psum | solution.py:62
  446.2 0.2 fusion.15
  446.4 0.2 fusion.30
  446.8 0.2 fusion.14
  447.3 0.2 fusion.13
  447.8 0.2 fusion.12
  448.0 0.2 fusion.52
  448.2 0.2 fusion.53
  448.4 0.2 fusion.11
  448.5 0.2 fusion.54
  448.8 0.2 convolution_divide_fusion
  449.0 1.6 fusion.55
  450.7 140.5 %all-reduce.7.cloned.1.call-done = f32[2,1152,32]{1,2,0:T(8,128)} async-done(((f32[2,1152,32]{1,2,0:T(8,128)}), f32[2,1152,32]{1,2,0:T(8,128)}) %all-reduce.7.cloned.1.call-update) | async-done | bytes 294928 | tf_op jit(solution)/shard_map/psum | solution.py:65
  591.1 4.4 subtract_convert_fusion
  595.6 0.7 fusion.32
  596.2 10.9 %all-gather = bf16[8,144,2]{1,2,0:T(2,128)(2,1)S(1)} all-gather(bf16[1,144,2]{1,2,0:T(2,128)(2,1)S(1)} %get-tuple-element.9), channel_id=1, replica_groups=mesh['rep'=16,'grp'=8] {'grp'}, dimensions={0}, use_global_device_ids=true | all-gather | bytes 5184 | tf_op jit(solution)/shard_map/all_gather | solution.py:74
  607.1 0.7 reshape.33
  607.8 23.3 %all-gather.3.cloned.1.call-done = bf16[2,1152,1152]{2,1,0:T(8,128)(2,1)} async-done(((bf16[2,144,1152]{2,1,0:T(8,128)(2,1)}), bf16[2,1152,1152]{2,1,0:T(8,128)(2,1)}) %all-gather.3.cloned.1.call-update) | async-done | bytes 5308432 | tf_op jit(solution)/shard_map/all_gather | solution.py:73
  631.1 5.3 copy.22
  (33 shorter events, 1.8 us)
Async XLA Ops:
  7.2 97.1 %copy-start = (f32[2,1152,32]{1,2,0:T(8,128)S(1)}, f32[2,1152,32]{1,2,0:T(8,128)}, u32[]{:S(2)}) copy-start(f32[2,1152,32]{1,2,0:T(8,128)} %param.15) | copy-start | bytes 884740
  7.2 53.6 %reduce-scatter.5.cloned.1.call-start = ((), (), s32[]{:S(2)}) async-start(), calls=%async_computation.3 | async-start | bytes 5971968 | tf_op jit(solution)/shard_map/reduce_scatter | solution.py:42
  19.8 83.0 %reduce-scatter.3.cloned.1.call-start = ((), (), s32[]{:S(2)}) async-start(), calls=%async_computation.2 | async-start | bytes 5971968 | tf_op jit(solution)/shard_map/reduce_scatter | solution.py:42
  32.5 70.3 %copy-start.1 = (f32[1,2,144,1152]{3,2,1,0:T(8,128)S(1)}, f32[1,2,144,1152]{3,2,1,0:T(8,128)}, u32[]{:S(2)}) copy-start(f32[1,2,144,1152]{3,2,1,0:T(8,128)} %param.12) | copy-start | bytes 3981316
  32.5 315.4 %all-reduce.5.cloned.1.call-start = ((), (), s32[]{:S(2)}) async-start(), calls=%async_computation.4 | async-start | bytes 589824 | tf_op jit(solution)/shard_map/psum | solution.py:65
  208.4 382.7 %all-reduce.7.cloned.1.call-start = ((), (), s32[]{:S(2)}) async-start(), calls=%async_computation.5 | async-start | bytes 589824 | tf_op jit(solution)/shard_map/psum | solution.py:65
  448.0 143.1 %copy-start.2 = (f32[2,144,1152]{2,1,0:T(8,128)S(1)}, f32[2,144,1152]{2,1,0:T(8,128)}, u32[]{:S(2)}) copy-start(f32[2,144,1152]{2,1,0:T(8,128)} %param.13) | copy-start | bytes 3981316
  450.6 145.0 %copy-start.3 = (f32[2,144]{1,0:T(2,128)S(1)}, f32[2,144]{1,0:T(2,128)}, u32[]{:S(2)}) copy-start(f32[2,144]{1,0:T(2,128)} %param.14) | copy-start | bytes 3460
  450.6 145.0 %copy-start.4 = (bf16[2,144]{1,0:T(2,128)(2,1)S(1)}, bf16[2,144]{1,0:T(2,128)(2,1)}, u32[]{:S(2)}) copy-start(bf16[2,144]{1,0:T(2,128)(2,1)} %param.11) | copy-start | bytes 1732
  450.6 180.5 %all-gather.3.cloned.1.call-start = ((), (), s32[]{:S(2)}) async-start(), calls=%async_computation.6 | async-start | bytes 5971968 | tf_op jit(solution)/shard_map/all_gather | solution.py:73
Sparse Core Ops, SparseCore 0:
  19.9 40.8 reduce-scatter.4
  63.2 39.5 reduce-scatter.2
  208.5 139.3 all-reduce.4
  450.7 140.3 all-reduce.6
  595.7 35.3 all-gather.2
